TPU v7x, 32 devices: a whole 2x2x4 slice. The times are simulated.
32 devices in a mesh: lat: 8 (over y, x, core), lon: 4 (over z).
Axes of the slice: x: 2, y: 2, z: 4, core: 2. Of those that a mesh axis runs over, the one named last changes fastest.
Arguments:
- snapshots: float32 [1024, 128, 512], P(None, 'lat', 'lon'), may hold values from -60 to 60
- land_sea: int32 [128, 512], P('lat', 'lon'), may hold values 0 or 1
- penalty: float32 [128, 512], P('lat', 'lon'), may hold values from 0.003 to 0.03
- initial_basis: float32 [64, 128, 512], P(None, 'lat', 'lon'), may hold values from -6 to 6
Outputs:
- leading_basis: float32 [64, 128, 512], P(None, 'lat', 'lon')
- rayleigh_matrix: float32 [64, 64], replicated
All inputs are finite; a program needn't handle non-finite values. No bound on the sum of `land_sea` on one device may be relied on, other than what follows from the above.
Results may differ from a plain program's by a relative error of at most 0.0003.
Values sent between devices are 32-bit elements; how exact they have to be, the bound alone decides.
A program may use at most 64 MiB of HBM per device.

v0:
```python
import functools

import jax
import jax.numpy as jnp
from jax import lax
from jax.experimental import pallas as pl
from jax.experimental.pallas import tpu as pltpu
from jax.sharding import PartitionSpec as P

STEPS = 2
MESH = pl.DeviceIdType.MESH
F32 = jnp.float32
BF16 = jnp.bfloat16
NT = (((1,), (1,)), ((), ()))
NN = (((1,), (0,)), ((), ()))


def dot_low(a, b, dims):
    return lax.dot_general(a, b, dims, preferred_element_type=F32)


def dot_full(a, b, dims):
    return lax.dot_general(
        a, b, dims, precision=lax.Precision.HIGHEST, preferred_element_type=F32
    )


def split(x):
    high = x.astype(BF16)
    return high, (x - high.astype(F32)).astype(BF16)


def split3(x):
    high = x.astype(BF16)
    rest = x - high.astype(F32)
    mid = rest.astype(BF16)
    return jnp.concatenate([high, mid, (rest - mid.astype(F32)).astype(BF16)], axis=0)


def fold_rows(x, k):
    return x[:k] + (x[k:2 * k] + x[2 * k:])


def products(left, right):
    k = left.shape[0] // 3
    x = fold_rows(dot_low(left, right, NT), k)
    return x[:, :k] + (x[:, k:2 * k] + x[:, 2 * k:])


def factor_parts(inverse):
    k = inverse.shape[0]
    parts = split3(inverse)
    return jnp.concatenate([parts, parts, parts], axis=1)


def times(parts, right):
    return fold_rows(dot_low(parts, right, NN), parts.shape[0] // 3)


def inverse_factor(gram):
    k = gram.shape[0]
    panel = 4
    rows = lax.broadcasted_iota(jnp.int32, (k, k), 0)
    cols = lax.broadcasted_iota(jnp.int32, (k, k), 1)
    eye = jnp.where(rows == cols, 1.0, 0.0).astype(F32)
    work = jnp.concatenate([gram, eye], axis=1)
    count = k // 8
    shape = (8, 2 * k)
    blocks = [work[8 * i:8 * i + 8] for i in range(count)]
    sub = lax.broadcasted_iota(jnp.int32, shape, 0)
    pivots = [jnp.zeros(shape, F32) for _ in range(count)]
    for j in range(0, k, panel):
        own, at = j // 8, j % 8
        row = [jnp.broadcast_to(blocks[own][at + a:at + a + 1, :], shape) for a in range(panel)]
        column = [
            [jnp.broadcast_to(blocks[i][:, j + a:j + a + 1], shape) for i in range(own, count)]
            for a in range(panel)
        ]
        corner = {
            (b, a): jnp.broadcast_to(column[a][0][at + b:at + b + 1, :], shape)
            for a in range(panel) for b in range(a, panel)
        }
        scaled = []
        for a in range(panel):
            pivot = corner[a, a]
            pivots[own] = jnp.where(sub == at + a, pivot, pivots[own])
            inverse = 1.0 / pivot
            scaled.append(row[a] * inverse)
            factor = {b: corner[b, a] * inverse for b in range(a + 1, panel)}
            for b in range(a + 1, panel):
                for c in range(b, panel):
                    corner[c, b] = corner[c, b] - factor[b] * corner[c, a]
            for b in range(a + 1, panel):
                row[b] = row[b] - factor[b] * row[a]
                column[b] = [y - factor[b] * x for x, y in zip(column[a], column[b])]
        for i in range(own, count):
            change = column[0][i - own] * scaled[0]
            for a in range(1, panel):
                change = change + column[a][i - own] * scaled[a]
            value = blocks[i] - change
            if i == own:
                value = jnp.where(sub >= at + panel, value, blocks[i])
                for a in range(panel):
                    value = jnp.where(sub == at + a, row[a], value)
            blocks[i] = value
    done = [blocks[i] * (1.0 / jnp.sqrt(pivots[i])) for i in range(count)]
    return jnp.concatenate(done, axis=0)[:, k:]


def kernel(
    n, m, points, s_hbm, land_ref, pen_ref, v_hbm, out_hbm, ray_ref,
    s_full, s_high, s_mid, field0, field1, field2, lap_ref, out_buf, v_split, acc,
    cbuf, rs, zr, fin, gl, gz, edge, halo,
    s_sem, v_sem, o_sem, rs_s, rs_r, z_s, z_r, ag_s, ag_r, gl_s, gl_r, gz_s, gz_r, h_s, h_r,
):
    lat = lax.axis_index("lat")
    lon = lax.axis_index("lon")
    t_count, a_count, b_count = s_hbm.shape
    k = v_hbm.shape[0]
    fields = (field0, field1, field2)
    shard = cbuf.shape[1] // n
    inverse_points = 1.0 / points
    pending = []

    def part(a):
        return pl.ds(a * b_count, b_count)

    loads = []
    for a in range(a_count):
        loads.append(pltpu.make_async_copy(v_hbm.at[:, a, :], out_buf.at[:, part(a)], v_sem.at[a]))
    for a in range(a_count):
        loads.append(pltpu.make_async_copy(s_hbm.at[:, a, :], s_full.at[:, part(a)], s_sem.at[a]))
    for copy in loads:
        copy.start()

    barrier = pltpu.get_barrier_semaphore()
    for d in range(1, n):
        pl.semaphore_signal(
            barrier, inc=1, device_id=(lax.rem(lat + d, n), lon), device_id_type=MESH
        )
    for e in range(1, m):
        pl.semaphore_signal(
            barrier, inc=1, device_id=(lat, lax.rem(lon + e, m)), device_id_type=MESH
        )
    pl.semaphore_wait(barrier, n + m - 2)

    def send(src, dst, s_s, s_r, where):
        copy = pltpu.make_async_remote_copy(
            src_ref=src, dst_ref=dst, send_sem=s_s, recv_sem=s_r,
            device_id=where, device_id_type=MESH,
        )
        copy.start()
        pending.append(copy)
        return copy

    def to_lat(d):
        return (lax.rem(lat + d, n), lon)

    def to_lon(e):
        return (lat, lax.rem(lon + e, m))

    lane = lax.broadcasted_iota(jnp.int32, (k, b_count), 1)

    def mask_row(a):
        return land_ref[a:a + 1, :].astype(F32)

    def start_halo(r):
        x = fields[r]
        packed = jnp.zeros((k, b_count), F32)
        for a in range(a_count):
            block = x[:, a * b_count:(a + 1) * b_count]
            low = block if a == 0 else pltpu.roll(block, a, axis=1)
            high = pltpu.roll(block, a_count + a + 1, axis=1)
            packed = jnp.where(lane == a, low, packed)
            packed = jnp.where(lane == a_count + a, high, packed)
        edge[r] = packed
        return [
            send(x.at[:, part(a_count - 1)], halo.at[r, 0], h_s.at[r, 0], h_r.at[r, 0], to_lat(1)),
            send(x.at[:, part(0)], halo.at[r, 1], h_s.at[r, 1], h_r.at[r, 1], to_lat(n - 1)),
            send(edge.at[r], halo.at[r, 2], h_s.at[r, 2], h_r.at[r, 2], to_lon(1)),
            send(edge.at[r], halo.at[r, 3], h_s.at[r, 3], h_r.at[r, 3], to_lon(m - 1)),
        ]

    def laplacian(r, copies):
        for copy in copies:
            copy.wait_recv()
        x = fields[r]
        above = jnp.where(lat > 0, halo[r, 0], 0.0)
        below = jnp.where(lat < n - 1, halo[r, 1], 0.0)
        west = jnp.where(lon > 0, halo[r, 2], 0.0)
        east = jnp.where(lon < m - 1, halo[r, 3], 0.0)
        for a in range(a_count):
            block = x[:, a * b_count:(a + 1) * b_count]
            up = above if a == 0 else x[:, (a - 1) * b_count:a * b_count]
            down = below if a == a_count - 1 else x[:, (a + 1) * b_count:(a + 2) * b_count]
            left = jnp.where(
                lane == 0, pltpu.roll(west, b_count - a_count - a, axis=1),
                pltpu.roll(block, 1, axis=1),
            )
            right = jnp.where(
                lane == b_count - 1, pltpu.roll(east, b_count - 1 - a, axis=1),
                pltpu.roll(block, b_count - 1, axis=1),
            )
            total = (down + up + right + left) - 4.0 * block
            lap_ref[:, a * b_count:(a + 1) * b_count] = total * pen_ref[a:a + 1, :]

    def store_field(r, a, value):
        x = value * mask_row(a)
        at = slice(a * b_count, (a + 1) * b_count)
        fields[r][:, at] = x
        v_split[:, at] = split3(x)

    def store_coeffs(r, block, value):
        for w in range(value.shape[1] // b_count):
            row = (block * (value.shape[1] // b_count) + w) * k
            cbuf[r, row:row + k, :] = value[:, w * b_count:(w + 1) * b_count]

    def start_scatter(r):
        copies = []
        for d in range(1, n):
            there = lax.rem(lat + d, n)
            rows = pl.ds(pl.multiple_of(there * shard, shard), shard)
            copies.append(
                send(cbuf.at[r, rows], rs.at[r, d], rs_s.at[r, d], rs_r.at[r, d], to_lat(d))
            )
        return copies

    def own_rows():
        return pl.ds(pl.multiple_of(lat * shard, shard), shard)

    def finish_scatter(r, copies):
        total = cbuf[r, own_rows(), :]
        for d, copy in enumerate(copies):
            copy.wait_recv()
            total = total + rs[r, d + 1]
        zr[r, lon] = total
        return [
            send(zr.at[r, lon], zr.at[r, lon], z_s.at[r, e], z_r.at[r, e], to_lon(e))
            for e in range(1, m)
        ]

    def start_gather(r, copies):
        for copy in copies:
            copy.wait_recv()
        total = zr[r, 0]
        for e in range(1, m):
            total = total + zr[r, e]
        fin[r, own_rows(), :] = total
        return [
            send(fin.at[r, own_rows()], fin.at[r, own_rows()], ag_s.at[r, d], ag_r.at[r, d], to_lat(d))
            for d in range(1, n)
        ]

    def finish_gather(r, copies):
        for copy in copies:
            copy.wait_recv()
        return jnp.concatenate(
            [fin[r, i * k:(i + 1) * k, :] for i in range(t_count // b_count)], axis=1
        )

    def start_gram(r, value):
        gl[r, lat] = value
        return [
            send(gl.at[r, lat], gl.at[r, lat], gl_s.at[r, d], gl_r.at[r, d], to_lat(d))
            for d in range(1, n)
        ]

    def middle_gram(r, copies):
        for copy in copies:
            copy.wait_recv()
        total = gl[r, 0]
        for d in range(1, n):
            total = total + gl[r, d]
        gz[r, lon] = total
        return [
            send(gz.at[r, lon], gz.at[r, lon], gz_s.at[r, e], gz_r.at[r, e], to_lon(e))
            for e in range(1, m)
        ]

    def finish_gram(r, copies):
        for copy in copies:
            copy.wait_recv()
        total = gz[r, 0]
        for e in range(1, m):
            total = total + gz[r, e]
        return total

    def project(r):
        width = 2 * b_count
        for block in range(t_count // width):
            rows = slice(block * width, (block + 1) * width)
            both = dot_low(v_split[:2 * k, :], s_high[rows, :], NT)
            rest = dot_low(v_split[:k, :], s_mid[rows, :], NT)
            store_coeffs(r, block, both[:k] + (both[k:] + rest))

    def expand(r, coeffs):
        high, mid = split(coeffs)
        stacked = jnp.concatenate([high, mid], axis=0)
        width = 2 * b_count
        for block in range(a_count // 2):
            at = slice(block * width, (block + 1) * width)
            both = dot_low(stacked, s_high[:, at], NN)
            rest = dot_low(high, s_mid[:, at], NN)
            value = (both[:k] + (both[k:] + rest)) * inverse_points + lap_ref[:, at]
            store_field(r, 2 * block, value[:, :b_count])
            store_field(r, 2 * block + 1, value[:, b_count:])

    for a in range(a_count):
        loads[a].wait()
        store_field(0, a, out_buf[:, a * b_count:(a + 1) * b_count])
    halo_copies = start_halo(0)
    width = 2 * b_count
    for block in range(a_count // 2):
        at = slice(block * width, (block + 1) * width)
        loads[a_count + 2 * block].wait()
        loads[a_count + 2 * block + 1].wait()
        high, mid = split(s_full[:, at])
        s_high[:, at] = high
        s_mid[:, at] = mid
        both = dot_low(v_split[:2 * k, at], high, NT)
        rest = dot_low(v_split[:k, at], mid, NT)
        value = both[:k] + (both[k:] + rest)
        if block == 0:
            acc[...] = value
        else:
            acc[...] += value
    store_coeffs(0, 0, acc[...])
    copies = start_scatter(0)
    laplacian(0, halo_copies)
    copies = finish_scatter(0, copies)
    copies = start_gather(0, copies)
    expand(1, finish_gather(0, copies))

    halo_copies = start_halo(1)
    gram = products(v_split[...], v_split[...]) * inverse_points
    gram_copies = start_gram(0, jnp.concatenate([gram, gram], axis=1))
    project(1)
    copies = start_scatter(1)
    gram_copies = middle_gram(0, gram_copies)
    laplacian(1, halo_copies)
    copies = finish_scatter(1, copies)
    parts = factor_parts(inverse_factor(finish_gram(0, gram_copies)[:, :k]))
    copies = start_gather(1, copies)
    lap_ref[...] = times(parts, split3(lap_ref[...]))
    expand(2, times(parts, split3(finish_gather(1, copies))))

    halo_copies = start_halo(2)
    project(2)
    copies = start_scatter(2)
    laplacian(2, halo_copies)
    gram = products(v_split[...], v_split[...]) * inverse_points
    rough = products(v_split[...], split3(lap_ref[...]))
    gram_copies = start_gram(1, jnp.concatenate([gram, rough], axis=1))
    copies = finish_scatter(2, copies)
    gram_copies = middle_gram(1, gram_copies)
    copies = start_gather(2, copies)
    both = finish_gram(1, gram_copies)
    inverse = inverse_factor(both[:, :k])
    parts = factor_parts(inverse)
    stores = []
    for a in range(a_count):
        at = slice(a * b_count, (a + 1) * b_count)
        out_buf[:, at] = times(parts, v_split[:, at])
        copy = pltpu.make_async_copy(out_buf.at[:, part(a)], out_hbm.at[:, a, :], o_sem.at[a])
        copy.start()
        stores.append(copy)
    coeffs = finish_gather(2, copies)
    coeffs = split3(coeffs)
    middle = products(coeffs, coeffs) * inverse_points + both[:, k:]
    ray_ref[...] = dot_full(dot_full(inverse, middle, NN), inverse, NT) * inverse_points
    for copy in stores:
        copy.wait()
    for copy in pending:
        copy.wait_send()


def local(snapshots, land_sea, penalty, initial_basis):
    n, m = lax.axis_size("lat"), lax.axis_size("lon")
    t, a, b = snapshots.shape
    k = initial_basis.shape[0]
    points = float(a * b * n * m)
    p = a * b
    rows = t * k // b
    shard = rows // n
    sem = pltpu.SemaphoreType.DMA
    vmem = pltpu.VMEM
    any_spec = pl.BlockSpec(memory_space=pl.ANY)
    vmem_spec = pl.BlockSpec(memory_space=pltpu.VMEM)
    return pl.pallas_call(
        functools.partial(kernel, n, m, points),
        out_shape=(
            jax.ShapeDtypeStruct((k, a, b), F32),
            jax.ShapeDtypeStruct((k, k), F32),
        ),
        in_specs=[any_spec, vmem_spec, vmem_spec, any_spec],
        out_specs=(any_spec, vmem_spec),
        scratch_shapes=[
            vmem((t, p), F32), vmem((t, p), BF16), vmem((t, p), BF16),
            vmem((k, p), F32), vmem((k, p), F32), vmem((k, p), F32),
            vmem((k, p), F32), vmem((k, p), F32), vmem((3 * k, p), BF16), vmem((k, t), F32),
            vmem((3, rows, b), F32), vmem((3, n, shard, b), F32), vmem((3, m, shard, b), F32),
            vmem((3, rows, b), F32), vmem((2, n, k, b), F32), vmem((2, m, k, b), F32),
            vmem((3, k, b), F32), vmem((3, 4, k, b), F32),
            sem((a,)), sem((a,)), sem((a,)),
            sem((3, n)), sem((3, n)), sem((3, m)), sem((3, m)), sem((3, n)), sem((3, n)),
            sem((2, n)), sem((2, n)), sem((2, m)), sem((2, m)), sem((3, 4)), sem((3, 4)),
        ],
        compiler_params=pltpu.CompilerParams(
            collective_id=0, has_side_effects=True, vmem_limit_bytes=60 * 1024 * 1024
        ),
        name="power_steps",
    )(snapshots, land_sea, penalty, initial_basis)


def solution(mesh):
    in_specs = (P(None, "lat", "lon"), P("lat", "lon"), P("lat", "lon"), P(None, "lat", "lon"))
    out_specs = (P(None, "lat", "lon"), P())
    return jax.shard_map(local, mesh=mesh, in_specs=in_specs, out_specs=out_specs, check_vma=False)
```

profile of v0, /device:TPU:0, one launch (start us, length us, event | category | flops | bytes accessed | tf_op | source)
XLA Modules:
  0.0 73.5 jit_solution(10788207939262459356)
XLA Ops:
  0.6 69.6 %power_steps.1 = (f32[64,16,128]{2,1,0:T(8,128)}, f32[64,64]{1,0:T(8,128)}) custom-call(f32[1024,16,128]{2,1,0:T(8,128)} %s_hbm.1, s32[16,128]{1,0:T(8,128)} %land_ref.1, f32[16,128]{1,0:T(8,128)} %pen_ref.1, f32[64,16,128]{2,1,0:T(8,128)} %v_hbm.1), custom_call_target="tpu_custom_call" | custom-call | tf_op jit(solution)/shard_map/power_steps/pallas_call | solution.py:389
  70.2 1.9 %copy.8 = f32[64,16,128]{2,1,0:T(8,128)} copy(f32[64,16,128]{2,1,0:T(8,128)} %get-tuple-element.4) | data formatting | bytes 1048576
  72.1 1.4 %copy.9 = f32[64,64]{1,0:T(8,128)} copy(f32[64,64]{1,0:T(8,128)} %get-tuple-element.5) | data formatting | bytes 32768
where the time goes:
time: 73.7 us; the launch traced here: 73.5 us
  Pallas kernels  69.6 us (94%)
  local copies, waits for them, and re-layouts  3.24 us (4%)
    pallas_call x1, Pallas kernels, local(): pl.pallas_call(functools.partial(kernel, n, m, points), out_shape=(jax.Sh...  69.6 us
    unnamed x2, local copies, waits for them, and re-layouts  3.24 us

commit v1 on v0

v1 whole, which is shorter than its diff:
```python
import functools

import jax
import jax.numpy as jnp
from jax import lax
from jax.experimental import pallas as pl
from jax.experimental.pallas import tpu as pltpu
from jax.sharding import PartitionSpec as P

STEPS = 2
MESH = pl.DeviceIdType.MESH
F32 = jnp.float32
BF16 = jnp.bfloat16
NT = (((1,), (1,)), ((), ()))
NN = (((1,), (0,)), ((), ()))


def dot_low(a, b, dims):
    return lax.dot_general(a, b, dims, preferred_element_type=F32)


def dot_full(a, b, dims):
    return lax.dot_general(
        a, b, dims, precision=lax.Precision.HIGHEST, preferred_element_type=F32
    )


def split(x):
    high = x.astype(BF16)
    return high, (x - high.astype(F32)).astype(BF16)


def split3(x):
    high = x.astype(BF16)
    rest = x - high.astype(F32)
    mid = rest.astype(BF16)
    return jnp.concatenate([high, mid, (rest - mid.astype(F32)).astype(BF16)], axis=0)


def fold_rows(x, k):
    return x[:k] + (x[k:2 * k] + x[2 * k:])


def products(left, right):
    k = left.shape[0] // 3
    x = fold_rows(dot_low(left, right, NT), k)
    return x[:, :k] + (x[:, k:2 * k] + x[:, 2 * k:])


def factor_parts(inverse):
    k = inverse.shape[0]
    parts = split3(inverse)
    return jnp.concatenate([parts, parts, parts], axis=1)


def times(parts, right):
    return fold_rows(dot_low(parts, right, NN), parts.shape[0] // 3)


def inverse_factor(gram):
    k = gram.shape[0]
    panel = 4
    rows = lax.broadcasted_iota(jnp.int32, (k, k), 0)
    cols = lax.broadcasted_iota(jnp.int32, (k, k), 1)
    eye = jnp.where(rows == cols, 1.0, 0.0).astype(F32)
    work = jnp.concatenate([gram, eye], axis=1)
    count = k // 8
    shape = (8, 2 * k)
    blocks = [work[8 * i:8 * i + 8] for i in range(count)]
    sub = lax.broadcasted_iota(jnp.int32, shape, 0)
    pivots = [jnp.zeros(shape, F32) for _ in range(count)]
    for j in range(0, k, panel):
        own, at = j // 8, j % 8
        row = [jnp.broadcast_to(blocks[own][at + a:at + a + 1, :], shape) for a in range(panel)]
        column = [
            [jnp.broadcast_to(blocks[i][:, j + a:j + a + 1], shape) for i in range(own, count)]
            for a in range(panel)
        ]
        corner = {
            (b, a): jnp.broadcast_to(column[a][0][at + b:at + b + 1, :], shape)
            for a in range(panel) for b in range(a, panel)
        }
        scaled = []
        for a in range(panel):
            pivot = corner[a, a]
            pivots[own] = jnp.where(sub == at + a, pivot, pivots[own])
            inverse = 1.0 / pivot
            scaled.append(row[a] * inverse)
            factor = {b: corner[b, a] * inverse for b in range(a + 1, panel)}
            for b in range(a + 1, panel):
                for c in range(b, panel):
                    corner[c, b] = corner[c, b] - factor[b] * corner[c, a]
            for b in range(a + 1, panel):
                row[b] = row[b] - factor[b] * row[a]
                column[b] = [y - factor[b] * x for x, y in zip(column[a], column[b])]
        for i in range(own, count):
            change = column[0][i - own] * scaled[0]
            for a in range(1, panel):
                change = change + column[a][i - own] * scaled[a]
            value = blocks[i] - change
            if i == own:
                value = jnp.where(sub >= at + panel, value, blocks[i])
                for a in range(panel):
                    value = jnp.where(sub == at + a, row[a], value)
            blocks[i] = value
    done = [blocks[i] * (1.0 / jnp.sqrt(pivots[i])) for i in range(count)]
    return jnp.concatenate(done, axis=0)[:, k:]


def pack(x):
    k = x.shape[0]
    return jnp.concatenate([x[:k // 2], x[k // 2:]], axis=1)


def unpack(x):
    k = x.shape[1] // 2
    return jnp.concatenate([x[:, :k], x[:, k:]], axis=0)


def flip(x, mask):
    result, bit = x, 1
    while bit <= mask:
        if mask & bit:
            result = result + bit - 2 * bit * lax.rem(lax.div(x, bit), 2)
        bit *= 2
    return result


def kernel(
    n, m, points, s_hbm, land_hbm, pen_hbm, v_hbm, out_ref, ray_ref,
    land_ref, pen_ref, s_full, s_high, s_mid, field0, field1, field2, lap_ref, v_split,
    cbuf, rs, zr, fin, g_in, gr, gz, g_out, plane, edge, halo, sides,
    c_sem, s_sem, v_sem, rs_s, rs_r, z_s, z_r, ag_s, ag_r, gr_s, gr_r, gz_s, gz_r, ga_s, ga_r,
    pl_s, pl_r, h_s, h_r,
):
    lat = lax.axis_index("lat")
    lon = lax.axis_index("lon")
    t_count, a_count, b_count = s_hbm.shape
    k = v_hbm.shape[0]
    fields = (field0, field1, field2)
    blocks = t_count // b_count
    pairs = blocks // 2
    per = n // blocks
    shard = k // per
    halves = 2
    part_rows = shard // halves
    wide = 2 * b_count
    gram_rows = k // blocks
    edge_groups = b_count // (2 * a_count)
    edge_rows = k // edge_groups
    inverse_points = 1.0 / points
    pending = []
    own_block = lax.div(lat, per)
    own_piece = lax.rem(lat, per)
    even = lax.rem(own_block, 2) == 0
    chip = lax.div(own_block, 2)

    def part(a):
        return pl.ds(a * b_count, b_count)

    def pair_rows(i):
        return pl.ds(pl.multiple_of(flip(chip, i) * wide, wide), wide)

    def piece_rows(piece, h=None):
        if h is None:
            return pl.ds(pl.multiple_of(piece * shard, shard), shard)
        return pl.ds(pl.multiple_of(piece * shard + h * part_rows, part_rows), part_rows)

    order = list(reversed(range(pairs)))
    groups = [order[g:g + 2] for g in range(0, pairs, 2)]
    land_copy = pltpu.make_async_copy(land_hbm, land_ref, c_sem.at[0])
    pen_copy = pltpu.make_async_copy(pen_hbm, pen_ref, c_sem.at[1])
    v_copies = [
        pltpu.make_async_copy(v_hbm.at[:, a, :], lap_ref.at[:, part(a)], v_sem.at[a])
        for a in range(a_count)
    ]
    s_copies = [
        [
            pltpu.make_async_copy(
                s_hbm.at[pair_rows(i), a, :], s_full.at[pair_rows(i), part(a)], s_sem.at[i, a]
            )
            for a in range(a_count)
        ]
        for i in range(pairs)
    ]
    land_copy.start()
    for copy in v_copies:
        copy.start()
    for i in reversed(range(pairs)):
        for copy in s_copies[i]:
            copy.start()
    pen_copy.start()

    barrier = pltpu.get_barrier_semaphore()
    for d in range(1, n):
        pl.semaphore_signal(barrier, inc=1, device_id=(flip(lat, d), lon), device_id_type=MESH)
    for e in range(1, m):
        pl.semaphore_signal(barrier, inc=1, device_id=(lat, flip(lon, e)), device_id_type=MESH)

    def send(src, dst, s_s, s_r, where):
        copy = pltpu.make_async_remote_copy(
            src_ref=src, dst_ref=dst, send_sem=s_s, recv_sem=s_r,
            device_id=where, device_id_type=MESH,
        )
        copy.start()
        pending.append(copy)
        return copy

    def to_lat(d):
        return (flip(lat, d), lon)

    def to_lon(e):
        return (lat, flip(lon, e))

    lane = lax.broadcasted_iota(jnp.int32, (k, b_count), 1)

    def mask_row(a):
        return land_ref[a:a + 1, :].astype(F32)

    def start_halo(r):
        x = fields[r]
        packed = jnp.zeros((k, b_count), F32)
        for a in range(a_count):
            block = x[:, a * b_count:(a + 1) * b_count]
            low = block if a == 0 else pltpu.roll(block, a, axis=1)
            high = pltpu.roll(block, a_count + a + 1, axis=1)
            packed = jnp.where(lane == a, low, packed)
            packed = jnp.where(lane == a_count + a, high, packed)
        narrow = packed[:edge_rows]
        for q in range(1, edge_groups):
            rows = packed[q * edge_rows:(q + 1) * edge_rows]
            narrow = narrow + pltpu.roll(rows, q * 2 * a_count, axis=1)
        edge[r] = narrow
        up, down = (lax.rem(lat + 1, n), lon), (lax.rem(lat + n - 1, n), lon)
        right, left = (lat, lax.rem(lon + 1, m)), (lat, lax.rem(lon + m - 1, m))
        return [
            send(x.at[:, part(a_count - 1)], halo.at[r, 0], h_s.at[r, 0], h_r.at[r, 0], up),
            send(x.at[:, part(0)], halo.at[r, 1], h_s.at[r, 1], h_r.at[r, 1], down),
            send(edge.at[r], sides.at[r, 0], h_s.at[r, 2], h_r.at[r, 2], right),
            send(edge.at[r], sides.at[r, 1], h_s.at[r, 3], h_r.at[r, 3], left),
        ]

    def widen(x):
        return jnp.concatenate(
            [x] + [
                pltpu.roll(x, b_count - q * 2 * a_count, axis=1) for q in range(1, edge_groups)
            ], axis=0,
        )

    def laplacian(r, copies):
        for copy in copies:
            copy.wait_recv()
        x = fields[r]
        above = jnp.where(lat > 0, halo[r, 0], 0.0)
        below = jnp.where(lat < n - 1, halo[r, 1], 0.0)
        west = jnp.where(lon > 0, widen(sides[r, 0]), 0.0)
        east = jnp.where(lon < m - 1, widen(sides[r, 1]), 0.0)
        for a in range(a_count):
            block = x[:, a * b_count:(a + 1) * b_count]
            up = above if a == 0 else x[:, (a - 1) * b_count:a * b_count]
            down = below if a == a_count - 1 else x[:, (a + 1) * b_count:(a + 2) * b_count]
            left = jnp.where(
                lane == 0, pltpu.roll(west, b_count - a_count - a, axis=1),
                pltpu.roll(block, 1, axis=1),
            )
            right = jnp.where(
                lane == b_count - 1, pltpu.roll(east, b_count - 1 - a, axis=1),
                pltpu.roll(block, b_count - 1, axis=1),
            )
            total = (down + up + right + left) - 4.0 * block
            lap_ref[:, a * b_count:(a + 1) * b_count] = total * pen_ref[a:a + 1, :]

    def store_field(r, a, value):
        x = value * mask_row(a)
        at = slice(a * b_count, (a + 1) * b_count)
        fields[r][:, at] = x
        v_split[:, at] = split3(x)

    def project_pair(r, i):
        rows = pair_rows(i)
        if r == 0:
            for copy in s_copies[i]:
                copy.wait()
            high, mid = split(s_full[rows, :])
            s_high[rows, :] = high
            s_mid[rows, :] = mid
        else:
            high, mid = s_high[rows, :], s_mid[rows, :]
        both = dot_low(v_split[:2 * k, :], high, NT)
        rest = dot_low(v_split[:k, :], mid, NT)
        value = both[:k] + (both[k:] + rest)
        low, up = value[:, :b_count], value[:, b_count:]
        cbuf[r, 2 * i] = jnp.where(even, low, up)
        cbuf[r, 2 * i + 1] = jnp.where(even, up, low)

    def send_pair(r, i, copies):
        for e in (1, 0):
            for q in range(per):
                d = (2 * i + e) * per + q
                if d:
                    rows = piece_rows(lax.rem(flip(lat, d), per))
                    copies[d] = send(
                        cbuf.at[r, 2 * i + e, rows], rs.at[r, d],
                        rs_s.at[r, d], rs_r.at[r, d], to_lat(d),
                    )

    def project(r):
        copies = {}
        for group in groups:
            for i in group:
                project_pair(r, i)
            for i in group:
                send_pair(r, i, copies)
        return copies

    def finish_scatter(r, copies):
        for d in sorted(copies, reverse=True):
            copies[d].wait_recv()
        result = []
        for h in range(halves):
            total = cbuf[r, 0, piece_rows(own_piece, h), :]
            at = slice(h * part_rows, (h + 1) * part_rows)
            for d in range(1, n):
                total = total + rs[r, d, at, :]
            zr[r, lon, at, :] = total
            result.append([
                send(
                    zr.at[r, lon, pl.ds(h * part_rows, part_rows)],
                    zr.at[r, lon, pl.ds(h * part_rows, part_rows)],
                    z_s.at[r, h, e], z_r.at[r, h, e], to_lon(e),
                )
                for e in reversed(range(1, m))
            ])
        return result

    def finish_lon(r, h, copies):
        for copy in copies[h]:
            copy.wait_recv()
        at = slice(h * part_rows, (h + 1) * part_rows)
        total = zr[r, 0, at, :]
        for e in range(1, m):
            total = total + zr[r, e, at, :]
        fin[r, 0, piece_rows(own_piece, h), :] = total

    def start_gather(r, copies):
        gathers = {}
        for h in range(halves):
            finish_lon(r, h, copies)
            rows = piece_rows(own_piece, h)
            for d in reversed(range(1, n)):
                gathers[h, d] = send(
                    fin.at[r, 0, rows], fin.at[r, d // per, rows],
                    ag_s.at[r, h, d], ag_r.at[r, h, d], to_lat(d),
                )
        return gathers

    def wait_block(block, copies):
        for q in range(per):
            d = block * per + q
            for h in range(halves):
                if d:
                    copies[h, d].wait_recv()

    def gram_piece(block):
        return pl.ds(pl.multiple_of(block * gram_rows, gram_rows), gram_rows)

    def start_gram(r, value):
        g_in[r] = jnp.concatenate([value, value], axis=1)
        gr[r, lat] = g_in[r, gram_piece(own_block), :]
        return [
            send(
                g_in.at[r, gram_piece(flip(own_block, d // per))], gr.at[r, lat],
                gr_s.at[r, d], gr_r.at[r, d], to_lat(d),
            )
            for d in reversed(range(1, n))
        ]

    def middle_gram(r, copies):
        for copy in copies:
            copy.wait_recv()
        total = gr[r, 0]
        for d in range(1, n):
            total = total + gr[r, d]
        gz[r, lon] = total
        return [
            send(gz.at[r, lon], gz.at[r, lon], gz_s.at[r, e], gz_r.at[r, e], to_lon(e))
            for e in reversed(range(1, m))
        ]

    def sum_gram(r, copies):
        for copy in copies:
            copy.wait_recv()
        total = gz[r, 0]
        for e in range(1, m):
            total = total + gz[r, e]
        return total

    def spread_gram(r, copies):
        g_out[r, gram_piece(own_block), :] = sum_gram(r, copies)
        rows = gram_piece(own_block)
        return [
            send(
                g_out.at[r, rows], g_out.at[r, rows],
                ga_s.at[r, block], ga_r.at[r, block], to_lat(block * per),
            )
            for block in reversed(range(1, blocks))
        ]

    def finish_gram(r, copies):
        for copy in copies:
            copy.wait_recv()
        return g_out[r, :, :k]

    def start_plane(value):
        plane[lat] = value
        return [
            send(plane.at[lat], plane.at[lat], pl_s.at[d], pl_r.at[d], to_lat(d))
            for d in reversed(range(1, n))
        ]

    def finish_plane(copies):
        for copy in copies:
            copy.wait_recv()
        total = plane[0]
        for d in range(1, n):
            total = total + plane[d]
        return total

    def expand(r, copies, parts=None):
        for i in range(pairs):
            for e in range(2):
                wait_block(2 * i + e, copies)
            near, far = fin[r - 1, 2 * i], fin[r - 1, 2 * i + 1]
            coeffs = jnp.concatenate(
                [jnp.where(even, near, far), jnp.where(even, far, near)], axis=1
            )
            high, mid = split(coeffs * inverse_points)
            stacked = jnp.concatenate([high, mid], axis=0)
            rows = pair_rows(i)
            for block in range(a_count // 2):
                at = slice(block * wide, (block + 1) * wide)
                both = dot_low(stacked, s_high[rows, at], NN)
                rest = dot_low(high, s_mid[rows, at], NN)
                value = lap_ref[:, at] + (both[:k] + (both[k:] + rest))
                if i < pairs - 1:
                    lap_ref[:, at] = value
                else:
                    if parts is not None:
                        value = times(parts, split3(value))
                    store_field(r, 2 * block, value[:, :b_count])
                    store_field(r, 2 * block + 1, value[:, b_count:])

    def gram():
        return products(v_split[...], v_split[...]) * inverse_points

    land_copy.wait()
    for a in range(a_count):
        v_copies[a].wait()
        store_field(0, a, lap_ref[:, a * b_count:(a + 1) * b_count])
    for i in groups[0]:
        project_pair(0, i)
    pl.semaphore_wait(barrier, n + m - 2)
    copies = {}
    for i in groups[0]:
        send_pair(0, i, copies)
    for group in groups[1:]:
        for i in group:
            project_pair(0, i)
        for i in group:
            send_pair(0, i, copies)
    halo_copies = start_halo(0)
    pen_copy.wait()
    copies = finish_scatter(0, copies)
    laplacian(0, halo_copies)
    copies = start_gather(0, copies)
    expand(1, copies)

    gram_copies = start_gram(0, gram())
    copies = project(1)
    halo_copies = start_halo(1)
    gram_copies = middle_gram(0, gram_copies)
    copies = finish_scatter(1, copies)
    gram_copies = spread_gram(0, gram_copies)
    laplacian(1, halo_copies)
    copies = start_gather(1, copies)
    parts = factor_parts(inverse_factor(finish_gram(0, gram_copies)))
    expand(2, copies, parts)

    gram_copies = start_gram(1, gram())
    halo_copies = start_halo(2)
    copies = project(2)
    gram_copies = middle_gram(1, gram_copies)
    laplacian(2, halo_copies)
    rough_copies = start_gram(2, products(v_split[...], split3(lap_ref[...])))
    copies = finish_scatter(2, copies)
    gram_copies = spread_gram(1, gram_copies)
    rough_copies = middle_gram(2, rough_copies)
    inverse = inverse_factor(finish_gram(1, gram_copies))
    rows = gram_piece(own_block)
    if per == 1:
        for h in range(halves):
            finish_lon(2, h, copies)
        coeffs = split3(fin[2, 0])
        middle = products(coeffs, coeffs) * inverse_points
        g_out[2] = jnp.concatenate([middle, middle], axis=1)
    else:
        g_out[2] = jnp.zeros((k, b_count), F32)
        copies = start_gather(2, copies)
    rough = jnp.where(own_piece == 0, sum_gram(2, rough_copies), 0.0)
    g_out[2, rows, :] = g_out[2, rows, :] + rough
    plane_copies = start_plane(pack(g_out[2, :, :k]))
    parts = factor_parts(inverse)
    for block in range(a_count // 2):
        at = slice(block * wide, (block + 1) * wide)
        out_ref[:, at] = times(parts, v_split[:, at])
    middle = unpack(finish_plane(plane_copies))
    if per > 1:
        for block in range(blocks):
            wait_block(block, copies)
        coeffs = split3(jnp.concatenate(
            [fin[2, flip(own_block, block)] for block in range(blocks)], axis=1
        ))
        middle = middle + products(coeffs, coeffs) * inverse_points
    ray_ref[...] = dot_full(dot_full(inverse, middle, NN), inverse, NT) * inverse_points
    for copy in pending:
        copy.wait_send()


def write_out(x_ref, ray_ref, out_hbm, ray_hbm, sems):
    a_count, b_count = out_hbm.shape[1:]
    copies = [pltpu.make_async_copy(ray_ref, ray_hbm, sems.at[a_count])]
    for a in range(a_count):
        at = pl.ds(a * b_count, b_count)
        copies.append(pltpu.make_async_copy(x_ref.at[:, at], out_hbm.at[:, a, :], sems.at[a]))
    for copy in copies:
        copy.start()
    for copy in copies:
        copy.wait()


def local(snapshots, land_sea, penalty, initial_basis):
    n, m = lax.axis_size("lat"), lax.axis_size("lon")
    t, a, b = snapshots.shape
    k = initial_basis.shape[0]
    points = float(a * b * n * m)
    p = a * b
    blocks = t // b
    shard = blocks * k // n
    sem = pltpu.SemaphoreType.DMA
    vmem = pltpu.VMEM
    any_spec = pl.BlockSpec(memory_space=pl.ANY)
    vmem_spec = pl.BlockSpec(memory_space=pltpu.VMEM)
    out, ray = pl.pallas_call(
        functools.partial(kernel, n, m, points),
        out_shape=(vmem((k, p), F32), vmem((k, k), F32)),
        in_specs=[any_spec, any_spec, any_spec, any_spec],
        out_specs=(vmem_spec, vmem_spec),
        scratch_shapes=[
            vmem((a, b), jnp.int32), vmem((a, b), F32),
            vmem((t, p), F32), vmem((t, p), BF16), vmem((t, p), BF16),
            vmem((k, p), F32), vmem((k, p), F32), vmem((k, p), F32),
            vmem((k, p), F32), vmem((3 * k, p), BF16),
            vmem((3, blocks, k, b), F32), vmem((3, n, shard, b), F32), vmem((3, m, shard, b), F32),
            vmem((3, blocks, k, b), F32), vmem((3, k, b), F32), vmem((3, n, k // blocks, b), F32),
            vmem((3, m, k // blocks, b), F32), vmem((3, k, b), F32), vmem((n, k // 2, b), F32),
            vmem((3, 2 * a * k // b, b), F32), vmem((3, 2, k, b), F32),
            vmem((3, 2, 2 * a * k // b, b), F32),
            sem((2,)), sem((blocks // 2, a)), sem((a,)),
            sem((3, n)), sem((3, n)), sem((3, 2, m)), sem((3, 2, m)), sem((3, 2, n)), sem((3, 2, n)),
            sem((3, n)), sem((3, n)), sem((3, m)), sem((3, m)), sem((3, blocks)), sem((3, blocks)),
            sem((n,)), sem((n,)), sem((3, 4)), sem((3, 4)),
        ],
        compiler_params=pltpu.CompilerParams(
            collective_id=0, has_side_effects=True, vmem_limit_bytes=60 * 1024 * 1024
        ),
        name="power_steps",
    )(snapshots, land_sea, penalty, initial_basis)
    return pl.pallas_call(
        write_out,
        out_shape=(jax.ShapeDtypeStruct((k, a, b), F32), jax.ShapeDtypeStruct((k, k), F32)),
        in_specs=[vmem_spec, vmem_spec],
        out_specs=(any_spec, any_spec),
        scratch_shapes=[sem((a + 1,))],
        name="write_out",
    )(
        pltpu.with_memory_space_constraint(out, pltpu.VMEM),
        pltpu.with_memory_space_constraint(ray, pltpu.VMEM),
    )


def solution(mesh):
    in_specs = (P(None, "lat", "lon"), P("lat", "lon"), P("lat", "lon"), P(None, "lat", "lon"))
    out_specs = (P(None, "lat", "lon"), P())
    return jax.shard_map(local, mesh=mesh, in_specs=in_specs, out_specs=out_specs, check_vma=False)
```

time: 73.7 us -> 64.8 us (0.88)
  Pallas kernels: 69.6 us -> 63.8 us
  local copies, waits for them, and re-layouts: 3.24 us -> 0 us
    pallas_call x1 -> x2, Pallas kernels: 69.6 us -> 63.8 us  [the longest x1 62.9 us: local(): pl.pallas_call(functools.partial(kernel, n, m, points), out_shape=(vmem((...]
    unnamed x2 -> x0, local copies, waits for them, and re-layouts: 3.24 us -> none
where the time goes in v1:
time: 64.8 us; the launch traced here: 64.6 us
  Pallas kernels  63.8 us (98%)
  between operations  0.8 us (1%)
    pallas_call x1, Pallas kernels, local(): pl.pallas_call(functools.partial(kernel, n, m, points), out_shape=(vmem((...  62.9 us

profile of v1, /device:TPU:0, one launch (start us, length us, event | category | flops | bytes accessed | tf_op | source)
XLA Modules:
  0.0 64.6 jit_solution(10250152607365941446)
XLA Ops:
  0.6 62.9 %power_steps.1 = (f32[64,2048]{1,0:T(8,128)S(1)}, f32[64,64]{1,0:T(8,128)S(1)}) custom-call(f32[1024,16,128]{2,1,0:T(8,128)} %s_hbm.1, s32[16,128]{1,0:T(8,128)} %land_hbm.1, f32[16,128]{1,0:T(8,128)} %pen_hbm.1, f32[64,16,128]{2,1,0:T(8,128)} %v_hbm.1), custom_call_target="tpu_custom_call" | custom-call | tf_op jit(solution)/shard_map/power_steps/pallas_call | solution.py:553
  63.5 0.9 %write_out.1 = (f32[64,16,128]{2,1,0:T(8,128)}, f32[64,64]{1,0:T(8,128)}) custom-call(f32[64,2048]{1,0:T(8,128)S(1)} %get-tuple-element.4.x_ref, f32[64,64]{1,0:T(8,128)S(1)} %get-tuple-element.5.ray_ref), custom_call_target="tpu_custom_call" | custom-call | tf_op jit(solution)/shard_map/write_out/pallas_call | solution.py:578

commit v2 on v1

--- a/solution.py
+++ b/solution.py
@@ -17,12 +17,6 @@
 
 def dot_low(a, b, dims):
     return lax.dot_general(a, b, dims, preferred_element_type=F32)
-
-
-def dot_full(a, b, dims):
-    return lax.dot_general(
-        a, b, dims, precision=lax.Precision.HIGHEST, preferred_element_type=F32
-    )
 
 
 def split(x):
@@ -128,7 +122,7 @@
 
 def kernel(
     n, m, points, s_hbm, land_hbm, pen_hbm, v_hbm, out_ref, ray_ref,
-    land_ref, pen_ref, s_full, s_high, s_mid, field0, field1, field2, lap_ref, v_split,
+    land_ref, pen_ref, s_full, s_high, s_mid, t_high, t_mid, field0, field1, field2, lap_ref, v_split,
     cbuf, rs, zr, fin, g_in, gr, gz, g_out, plane, edge, halo, sides,
     c_sem, s_sem, v_sem, rs_s, rs_r, z_s, z_r, ag_s, ag_r, gr_s, gr_r, gz_s, gz_r, ga_s, ga_r,
     pl_s, pl_r, h_s, h_r,
@@ -166,6 +160,7 @@
             return pl.ds(pl.multiple_of(piece * shard, shard), shard)
         return pl.ds(pl.multiple_of(piece * shard + h * part_rows, part_rows), part_rows)
 
+    half_rows = a_count // 2
     order = list(reversed(range(pairs)))
     groups = [order[g:g + 2] for g in range(0, pairs, 2)]
     land_copy = pltpu.make_async_copy(land_hbm, land_ref, c_sem.at[0])
@@ -186,9 +181,11 @@
     land_copy.start()
     for copy in v_copies:
         copy.start()
-    for i in reversed(range(pairs)):
-        for copy in s_copies[i]:
-            copy.start()
+    for group in groups:
+        for h in range(2):
+            for i in group:
+                for copy in s_copies[i][h * half_rows:(h + 1) * half_rows]:
+                    copy.start()
     pen_copy.start()
 
     barrier = pltpu.get_barrier_semaphore()
@@ -276,22 +273,43 @@
         fields[r][:, at] = x
         v_split[:, at] = split3(x)
 
-    def project_pair(r, i):
-        rows = pair_rows(i)
-        if r == 0:
-            for copy in s_copies[i]:
-                copy.wait()
-            high, mid = split(s_full[rows, :])
-            s_high[rows, :] = high
-            s_mid[rows, :] = mid
-        else:
-            high, mid = s_high[rows, :], s_mid[rows, :]
-        both = dot_low(v_split[:2 * k, :], high, NT)
-        rest = dot_low(v_split[:k, :], mid, NT)
+    def store_pair(r, i, both, rest):
         value = both[:k] + (both[k:] + rest)
         low, up = value[:, :b_count], value[:, b_count:]
         cbuf[r, 2 * i] = jnp.where(even, low, up)
         cbuf[r, 2 * i + 1] = jnp.where(even, up, low)
+
+    def project_first(group):
+        sums = {}
+        for h in range(2):
+            at = slice(h * half_rows * b_count, (h + 1) * half_rows * b_count)
+            for i in group:
+                for copy in s_copies[i][h * half_rows:(h + 1) * half_rows]:
+                    copy.wait()
+            for i in group:
+                rows = pair_rows(i)
+                high, mid = split(s_full[rows, at])
+                s_high[rows, at] = high
+                s_mid[rows, at] = mid
+                both = dot_low(v_split[:2 * k, at], high, NT)
+                rest = dot_low(v_split[:k, at], mid, NT)
+                if h:
+                    store_pair(0, i, sums[i][0] + both, sums[i][1] + rest)
+                else:
+                    sums[i] = both, rest
+
+    def project_pair(r, i):
+        rows = pair_rows(i)
+        both = dot_low(v_split[:2 * k, :], t_high[:, rows], NN)
+        rest = dot_low(v_split[:k, :], t_mid[:, rows], NN)
+        store_pair(r, i, both, rest)
+
+    def turn(source, target):
+        for i in range(pairs):
+            rows = slice(i * wide, (i + 1) * wide)
+            for block in range(a_count // 2):
+                at = slice(block * wide, (block + 1) * wide)
+                target[at, rows] = source[rows, at].T
 
     def send_pair(r, i, copies):
         for e in (1, 0):
@@ -426,29 +444,28 @@
             total = total + plane[d]
         return total
 
-    def expand(r, copies, parts=None):
-        for i in range(pairs):
-            for e in range(2):
-                wait_block(2 * i + e, copies)
-            near, far = fin[r - 1, 2 * i], fin[r - 1, 2 * i + 1]
-            coeffs = jnp.concatenate(
-                [jnp.where(even, near, far), jnp.where(even, far, near)], axis=1
-            )
-            high, mid = split(coeffs * inverse_points)
-            stacked = jnp.concatenate([high, mid], axis=0)
-            rows = pair_rows(i)
-            for block in range(a_count // 2):
-                at = slice(block * wide, (block + 1) * wide)
-                both = dot_low(stacked, s_high[rows, at], NN)
-                rest = dot_low(high, s_mid[rows, at], NN)
-                value = lap_ref[:, at] + (both[:k] + (both[k:] + rest))
-                if i < pairs - 1:
-                    lap_ref[:, at] = value
-                else:
-                    if parts is not None:
-                        value = times(parts, split3(value))
-                    store_field(r, 2 * block, value[:, :b_count])
-                    store_field(r, 2 * block + 1, value[:, b_count:])
+    def expand_pair(r, i, copies, parts=None):
+        for e in range(2):
+            wait_block(2 * i + e, copies)
+        near, far = fin[r - 1, 2 * i], fin[r - 1, 2 * i + 1]
+        coeffs = jnp.concatenate(
+            [jnp.where(even, near, far), jnp.where(even, far, near)], axis=1
+        )
+        high, mid = split(coeffs * inverse_points)
+        stacked = jnp.concatenate([high, mid], axis=0)
+        rows = pair_rows(i)
+        for block in range(a_count // 2):
+            at = slice(block * wide, (block + 1) * wide)
+            both = dot_low(stacked, s_high[rows, at], NN)
+            rest = dot_low(high, s_mid[rows, at], NN)
+            value = lap_ref[:, at] + (both[:k] + (both[k:] + rest))
+            if i < pairs - 1:
+                lap_ref[:, at] = value
+            else:
+                if parts is not None:
+                    value = times(parts, split3(value))
+                store_field(r, 2 * block, value[:, :b_count])
+                store_field(r, 2 * block + 1, value[:, b_count:])
 
     def gram():
         return products(v_split[...], v_split[...]) * inverse_points
@@ -457,23 +474,24 @@
     for a in range(a_count):
         v_copies[a].wait()
         store_field(0, a, lap_ref[:, a * b_count:(a + 1) * b_count])
-    for i in groups[0]:
-        project_pair(0, i)
+    project_first(groups[0])
     pl.semaphore_wait(barrier, n + m - 2)
     copies = {}
     for i in groups[0]:
         send_pair(0, i, copies)
     for group in groups[1:]:
-        for i in group:
-            project_pair(0, i)
+        project_first(group)
         for i in group:
             send_pair(0, i, copies)
     halo_copies = start_halo(0)
     pen_copy.wait()
+    turn(s_high, t_high)
     copies = finish_scatter(0, copies)
+    turn(s_mid, t_mid)
     laplacian(0, halo_copies)
     copies = start_gather(0, copies)
-    expand(1, copies)
+    for i in range(pairs):
+        expand_pair(1, i, copies)
 
     gram_copies = start_gram(0, gram())
     copies = project(1)
@@ -483,8 +501,10 @@
     gram_copies = spread_gram(0, gram_copies)
     laplacian(1, halo_copies)
     copies = start_gather(1, copies)
+    expand_pair(2, 0, copies)
     parts = factor_parts(inverse_factor(finish_gram(0, gram_copies)))
-    expand(2, copies, parts)
+    for i in range(1, pairs):
+        expand_pair(2, i, copies, parts)
 
     gram_copies = start_gram(1, gram())
     halo_copies = start_halo(2)
@@ -495,7 +515,6 @@
     copies = finish_scatter(2, copies)
     gram_copies = spread_gram(1, gram_copies)
     rough_copies = middle_gram(2, rough_copies)
-    inverse = inverse_factor(finish_gram(1, gram_copies))
     rows = gram_piece(own_block)
     if per == 1:
         for h in range(halves):
@@ -509,6 +528,7 @@
     rough = jnp.where(own_piece == 0, sum_gram(2, rough_copies), 0.0)
     g_out[2, rows, :] = g_out[2, rows, :] + rough
     plane_copies = start_plane(pack(g_out[2, :, :k]))
+    inverse = inverse_factor(finish_gram(1, gram_copies))
     parts = factor_parts(inverse)
     for block in range(a_count // 2):
         at = slice(block * wide, (block + 1) * wide)
@@ -521,7 +541,8 @@
             [fin[2, flip(own_block, block)] for block in range(blocks)], axis=1
         ))
         middle = middle + products(coeffs, coeffs) * inverse_points
-    ray_ref[...] = dot_full(dot_full(inverse, middle, NN), inverse, NT) * inverse_points
+    half = times(parts, split3(middle))
+    ray_ref[...] = products(split3(half), split3(inverse)) * inverse_points
     for copy in pending:
         copy.wait_send()
 
@@ -558,6 +579,7 @@
         scratch_shapes=[
             vmem((a, b), jnp.int32), vmem((a, b), F32),
             vmem((t, p), F32), vmem((t, p), BF16), vmem((t, p), BF16),
+            vmem((p, t), BF16), vmem((p, t), BF16),
             vmem((k, p), F32), vmem((k, p), F32), vmem((k, p), F32),
             vmem((k, p), F32), vmem((3 * k, p), BF16),
             vmem((3, blocks, k, b), F32), vmem((3, n, shard, b), F32), vmem((3, m, shard, b), F32),

time: 64.8 us -> 62.4 us (0.963)
  Pallas kernels: 63.8 us -> 61.5 us
    pallas_call x1, Pallas kernels: 62.9 us -> 60.5 us  [local(): pl.pallas_call(functools.partial(kernel, n, m, points), out_shape=(vmem((...]
where the time goes in v2:
time: 62.4 us; the launch traced here: 62.3 us
  Pallas kernels  61.5 us (99%)
  between operations  0.8 us (1%)
    pallas_call x1, Pallas kernels, local(): pl.pallas_call(functools.partial(kernel, n, m, points), out_shape=(vmem((...  60.5 us

profile of v2, /device:TPU:0, one launch (start us, length us, event | category | flops | bytes accessed | tf_op | source)
XLA Modules:
  0.0 62.3 jit_solution(12128667828685847755)
XLA Ops:
  0.6 60.5 %power_steps.1 = (f32[64,2048]{1,0:T(8,128)S(1)}, f32[64,64]{1,0:T(8,128)S(1)}) custom-call(f32[1024,16,128]{2,1,0:T(8,128)} %s_hbm.1, s32[16,128]{1,0:T(8,128)} %land_hbm.1, f32[16,128]{1,0:T(8,128)} %pen_hbm.1, f32[64,16,128]{2,1,0:T(8,128)} %v_hbm.1), custom_call_target="tpu_custom_call" | custom-call | tf_op jit(solution)/shard_map/power_steps/pallas_call | solution.py:574
  61.2 0.9 %write_out.1 = (f32[64,16,128]{2,1,0:T(8,128)}, f32[64,64]{1,0:T(8,128)}) custom-call(f32[64,2048]{1,0:T(8,128)S(1)} %get-tuple-element.4.x_ref, f32[64,64]{1,0:T(8,128)S(1)} %get-tuple-element.5.ray_ref), custom_call_target="tpu_custom_call" | custom-call | tf_op jit(solution)/shard_map/write_out/pallas_call | solution.py:600

commit v3 on v2

--- a/solution.py
+++ b/solution.py
@@ -123,9 +123,8 @@
 def kernel(
     n, m, points, s_hbm, land_hbm, pen_hbm, v_hbm, out_ref, ray_ref,
     land_ref, pen_ref, s_full, s_high, s_mid, t_high, t_mid, field0, field1, field2, lap_ref, v_split,
-    cbuf, rs, zr, fin, g_in, gr, gz, g_out, plane, edge, halo, sides,
-    c_sem, s_sem, v_sem, rs_s, rs_r, z_s, z_r, ag_s, ag_r, gr_s, gr_r, gz_s, gz_r, ga_s, ga_r,
-    pl_s, pl_r, h_s, h_r,
+    cbuf, rs, zr, fin, g_in, gr, gz, g_out, plane, edge, halo,
+    c_sem, s_sem, rs_s, rs_r, z_s, z_r, ag_s, ag_r, gr_s, gr_r, gz_s, gz_r, ga_s, ga_r, h_s, h_r,
 ):
     lat = lax.axis_index("lat")
     lon = lax.axis_index("lon")
@@ -139,11 +138,11 @@
     halves = 2
     part_rows = shard // halves
     wide = 2 * b_count
+    half_rows = a_count // 2
     gram_rows = k // blocks
     edge_groups = b_count // (2 * a_count)
     edge_rows = k // edge_groups
     inverse_points = 1.0 / points
-    pending = []
     own_block = lax.div(lat, per)
     own_piece = lax.rem(lat, per)
     even = lax.rem(own_block, 2) == 0
@@ -160,19 +159,18 @@
             return pl.ds(pl.multiple_of(piece * shard, shard), shard)
         return pl.ds(pl.multiple_of(piece * shard + h * part_rows, part_rows), part_rows)
 
-    half_rows = a_count // 2
     order = list(reversed(range(pairs)))
     groups = [order[g:g + 2] for g in range(0, pairs, 2)]
     land_copy = pltpu.make_async_copy(land_hbm, land_ref, c_sem.at[0])
     pen_copy = pltpu.make_async_copy(pen_hbm, pen_ref, c_sem.at[1])
     v_copies = [
-        pltpu.make_async_copy(v_hbm.at[:, a, :], lap_ref.at[:, part(a)], v_sem.at[a])
+        pltpu.make_async_copy(v_hbm.at[:, a, :], lap_ref.at[:, part(a)], c_sem.at[2])
         for a in range(a_count)
     ]
     s_copies = [
         [
             pltpu.make_async_copy(
-                s_hbm.at[pair_rows(i), a, :], s_full.at[pair_rows(i), part(a)], s_sem.at[i, a]
+                s_hbm.at[pair_rows(i), a, :], s_full.at[pair_rows(i), part(a)], s_sem.at[i, a // half_rows]
             )
             for a in range(a_count)
         ]
@@ -200,8 +198,9 @@
             device_id=where, device_id_type=MESH,
         )
         copy.start()
-        pending.append(copy)
-        return copy
+
+    def arrived(ref, sem):
+        pltpu.make_async_copy(ref, ref, sem).wait()
 
     def to_lat(d):
         return (flip(lat, d), lon)
@@ -230,12 +229,12 @@
         edge[r] = narrow
         up, down = (lax.rem(lat + 1, n), lon), (lax.rem(lat + n - 1, n), lon)
         right, left = (lat, lax.rem(lon + 1, m)), (lat, lax.rem(lon + m - 1, m))
-        return [
-            send(x.at[:, part(a_count - 1)], halo.at[r, 0], h_s.at[r, 0], h_r.at[r, 0], up),
-            send(x.at[:, part(0)], halo.at[r, 1], h_s.at[r, 1], h_r.at[r, 1], down),
-            send(edge.at[r], sides.at[r, 0], h_s.at[r, 2], h_r.at[r, 2], right),
-            send(edge.at[r], sides.at[r, 1], h_s.at[r, 3], h_r.at[r, 3], left),
-        ]
+        first, second = pl.ds(0, k), pl.ds(k, k)
+        third, fourth = pl.ds(2 * k, edge_rows), pl.ds(2 * k + edge_rows, edge_rows)
+        send(x.at[:, part(a_count - 1)], halo.at[r, first], h_s.at[r], h_r.at[r], up)
+        send(x.at[:, part(0)], halo.at[r, second], h_s.at[r], h_r.at[r], down)
+        send(edge.at[r], halo.at[r, third], h_s.at[r], h_r.at[r], right)
+        send(edge.at[r], halo.at[r, fourth], h_s.at[r], h_r.at[r], left)
 
     def widen(x):
         return jnp.concatenate(
@@ -244,14 +243,13 @@
             ], axis=0,
         )
 
-    def laplacian(r, copies):
-        for copy in copies:
-            copy.wait_recv()
+    def laplacian(r):
+        arrived(halo.at[r], h_r.at[r])
         x = fields[r]
-        above = jnp.where(lat > 0, halo[r, 0], 0.0)
-        below = jnp.where(lat < n - 1, halo[r, 1], 0.0)
-        west = jnp.where(lon > 0, widen(sides[r, 0]), 0.0)
-        east = jnp.where(lon < m - 1, widen(sides[r, 1]), 0.0)
+        above = jnp.where(lat > 0, halo[r, :k, :], 0.0)
+        below = jnp.where(lat < n - 1, halo[r, k:2 * k, :], 0.0)
+        west = jnp.where(lon > 0, widen(halo[r, 2 * k:2 * k + edge_rows, :]), 0.0)
+        east = jnp.where(lon < m - 1, widen(halo[r, 2 * k + edge_rows:, :]), 0.0)
         for a in range(a_count):
             block = x[:, a * b_count:(a + 1) * b_count]
             up = above if a == 0 else x[:, (a - 1) * b_count:a * b_count]
@@ -284,8 +282,8 @@
         for h in range(2):
             at = slice(h * half_rows * b_count, (h + 1) * half_rows * b_count)
             for i in group:
-                for copy in s_copies[i][h * half_rows:(h + 1) * half_rows]:
-                    copy.wait()
+                cols = pl.ds(h * half_rows * b_count, half_rows * b_count)
+                arrived(s_full.at[pair_rows(i), cols], s_sem.at[i, h])
             for i in group:
                 rows = pair_rows(i)
                 high, mid = split(s_full[rows, at])
@@ -311,73 +309,63 @@
                 at = slice(block * wide, (block + 1) * wide)
                 target[at, rows] = source[rows, at].T
 
-    def send_pair(r, i, copies):
+    def send_pair(r, i):
         for e in (1, 0):
             for q in range(per):
                 d = (2 * i + e) * per + q
                 if d:
                     rows = piece_rows(lax.rem(flip(lat, d), per))
-                    copies[d] = send(
+                    send(
                         cbuf.at[r, 2 * i + e, rows], rs.at[r, d],
-                        rs_s.at[r, d], rs_r.at[r, d], to_lat(d),
+                        rs_s.at[r], rs_r.at[r], to_lat(d),
                     )
 
     def project(r):
-        copies = {}
         for group in groups:
             for i in group:
                 project_pair(r, i)
             for i in group:
-                send_pair(r, i, copies)
-        return copies
-
-    def finish_scatter(r, copies):
-        for d in sorted(copies, reverse=True):
-            copies[d].wait_recv()
-        result = []
+                send_pair(r, i)
+
+    def finish_scatter(r):
+        arrived(rs.at[r, pl.ds(1, n - 1)], rs_r.at[r])
         for h in range(halves):
             total = cbuf[r, 0, piece_rows(own_piece, h), :]
             at = slice(h * part_rows, (h + 1) * part_rows)
             for d in range(1, n):
                 total = total + rs[r, d, at, :]
             zr[r, lon, at, :] = total
-            result.append([
-                send(
-                    zr.at[r, lon, pl.ds(h * part_rows, part_rows)],
-                    zr.at[r, lon, pl.ds(h * part_rows, part_rows)],
-                    z_s.at[r, h, e], z_r.at[r, h, e], to_lon(e),
-                )
-                for e in reversed(range(1, m))
-            ])
-        return result
-
-    def finish_lon(r, h, copies):
-        for copy in copies[h]:
-            copy.wait_recv()
+            own = zr.at[r, lon, pl.ds(h * part_rows, part_rows)]
+            for e in reversed(range(1, m)):
+                send(own, own, z_s.at[r], z_r.at[r, h], to_lon(e))
+
+    def finish_lon(r, h):
+        arrived(zr.at[r, pl.ds(1, m - 1), pl.ds(h * part_rows, part_rows)], z_r.at[r, h])
         at = slice(h * part_rows, (h + 1) * part_rows)
         total = zr[r, 0, at, :]
         for e in range(1, m):
             total = total + zr[r, e, at, :]
-        fin[r, 0, piece_rows(own_piece, h), :] = total
-
-    def start_gather(r, copies):
-        gathers = {}
+        fin[r, own_piece, at, :] = total
+
+    def start_gather(r):
         for h in range(halves):
-            finish_lon(r, h, copies)
-            rows = piece_rows(own_piece, h)
+            finish_lon(r, h)
+            rows = pl.ds(h * part_rows, part_rows)
             for d in reversed(range(1, n)):
-                gathers[h, d] = send(
-                    fin.at[r, 0, rows], fin.at[r, d // per, rows],
-                    ag_s.at[r, h, d], ag_r.at[r, h, d], to_lat(d),
+                block = d // per
+                send(
+                    fin.at[r, own_piece, rows], fin.at[r, block * per + own_piece, rows],
+                    ag_s.at[r], ag_r.at[r, block // 2], to_lat(d),
                 )
-        return gathers
-
-    def wait_block(block, copies):
-        for q in range(per):
-            d = block * per + q
-            for h in range(halves):
-                if d:
-                    copies[h, d].wait_recv()
+
+    def wait_pair(r, i):
+        if i:
+            arrived(fin.at[r, pl.ds(2 * i * per, 2 * per)], ag_r.at[r, i])
+        else:
+            arrived(fin.at[r, pl.ds(1, 2 * per - 1)], ag_r.at[r, i])
+
+    def load_block(r, block):
+        return fin[r, block * per:(block + 1) * per].reshape(k, b_count)
 
     def gram_piece(block):
         return pl.ds(pl.multiple_of(block * gram_rows, gram_rows), gram_rows)
@@ -385,69 +373,58 @@
     def start_gram(r, value):
         g_in[r] = jnp.concatenate([value, value], axis=1)
         gr[r, lat] = g_in[r, gram_piece(own_block), :]
-        return [
+        for d in reversed(range(1, n)):
             send(
                 g_in.at[r, gram_piece(flip(own_block, d // per))], gr.at[r, lat],
-                gr_s.at[r, d], gr_r.at[r, d], to_lat(d),
+                gr_s.at[r], gr_r.at[r], to_lat(d),
             )
-            for d in reversed(range(1, n))
-        ]
-
-    def middle_gram(r, copies):
-        for copy in copies:
-            copy.wait_recv()
+
+    def middle_gram(r):
+        arrived(gr.at[r, pl.ds(1, n - 1)], gr_r.at[r])
         total = gr[r, 0]
         for d in range(1, n):
             total = total + gr[r, d]
         gz[r, lon] = total
-        return [
-            send(gz.at[r, lon], gz.at[r, lon], gz_s.at[r, e], gz_r.at[r, e], to_lon(e))
-            for e in reversed(range(1, m))
-        ]
-
-    def sum_gram(r, copies):
-        for copy in copies:
-            copy.wait_recv()
+        for e in reversed(range(1, m)):
+            send(gz.at[r, lon], gz.at[r, lon], gz_s.at[r], gz_r.at[r], to_lon(e))
+
+    def sum_gram(r):
+        arrived(gz.at[r, pl.ds(1, m - 1)], gz_r.at[r])
         total = gz[r, 0]
         for e in range(1, m):
             total = total + gz[r, e]
         return total
 
-    def spread_gram(r, copies):
-        g_out[r, gram_piece(own_block), :] = sum_gram(r, copies)
+    def spread_gram(r):
         rows = gram_piece(own_block)
-        return [
+        g_out[r, rows, :] = sum_gram(r)
+        for block in reversed(range(1, blocks)):
             send(
-                g_out.at[r, rows], g_out.at[r, rows],
-                ga_s.at[r, block], ga_r.at[r, block], to_lat(block * per),
+                g_out.at[r, rows], g_out.at[r, rows], ga_s.at[r], ga_r.at[r], to_lat(block * per)
             )
-            for block in reversed(range(1, blocks))
-        ]
-
-    def finish_gram(r, copies):
-        for copy in copies:
-            copy.wait_recv()
+
+    def other_pieces(r):
+        return g_out.at[r, pl.ds(gram_rows, k - gram_rows)]
+
+    def finish_gram(r):
+        arrived(other_pieces(r), ga_r.at[r])
         return g_out[r, :, :k]
 
     def start_plane(value):
         plane[lat] = value
-        return [
-            send(plane.at[lat], plane.at[lat], pl_s.at[d], pl_r.at[d], to_lat(d))
-            for d in reversed(range(1, n))
-        ]
-
-    def finish_plane(copies):
-        for copy in copies:
-            copy.wait_recv()
+        for d in reversed(range(1, n)):
+            send(plane.at[lat], plane.at[lat], c_sem.at[3], c_sem.at[4], to_lat(d))
+
+    def finish_plane():
+        arrived(plane.at[pl.ds(1, n - 1)], c_sem.at[4])
         total = plane[0]
         for d in range(1, n):
             total = total + plane[d]
         return total
 
-    def expand_pair(r, i, copies, parts=None):
-        for e in range(2):
-            wait_block(2 * i + e, copies)
-        near, far = fin[r - 1, 2 * i], fin[r - 1, 2 * i + 1]
+    def expand_pair(r, i, parts=None):
+        wait_pair(r - 1, i)
+        near, far = load_block(r - 1, 2 * i), load_block(r - 1, 2 * i + 1)
         coeffs = jnp.concatenate(
             [jnp.where(even, near, far), jnp.where(even, far, near)], axis=1
         )
@@ -471,92 +448,102 @@
         return products(v_split[...], v_split[...]) * inverse_points
 
     land_copy.wait()
+    arrived(lap_ref, c_sem.at[2])
     for a in range(a_count):
-        v_copies[a].wait()
         store_field(0, a, lap_ref[:, a * b_count:(a + 1) * b_count])
     project_first(groups[0])
     pl.semaphore_wait(barrier, n + m - 2)
-    copies = {}
     for i in groups[0]:
-        send_pair(0, i, copies)
+        send_pair(0, i)
     for group in groups[1:]:
         project_first(group)
         for i in group:
-            send_pair(0, i, copies)
-    halo_copies = start_halo(0)
+            send_pair(0, i)
+    start_halo(0)
     pen_copy.wait()
     turn(s_high, t_high)
-    copies = finish_scatter(0, copies)
+    finish_scatter(0)
     turn(s_mid, t_mid)
-    laplacian(0, halo_copies)
-    copies = start_gather(0, copies)
+    laplacian(0)
+    start_gather(0)
     for i in range(pairs):
-        expand_pair(1, i, copies)
-
-    gram_copies = start_gram(0, gram())
-    copies = project(1)
-    halo_copies = start_halo(1)
-    gram_copies = middle_gram(0, gram_copies)
-    copies = finish_scatter(1, copies)
-    gram_copies = spread_gram(0, gram_copies)
-    laplacian(1, halo_copies)
-    copies = start_gather(1, copies)
-    expand_pair(2, 0, copies)
-    parts = factor_parts(inverse_factor(finish_gram(0, gram_copies)))
+        expand_pair(1, i)
+
+    start_gram(0, gram())
+    project(1)
+    start_halo(1)
+    middle_gram(0)
+    finish_scatter(1)
+    spread_gram(0)
+    laplacian(1)
+    start_gather(1)
+    expand_pair(2, 0)
+    parts = factor_parts(inverse_factor(finish_gram(0)))
     for i in range(1, pairs):
-        expand_pair(2, i, copies, parts)
-
-    gram_copies = start_gram(1, gram())
-    halo_copies = start_halo(2)
-    copies = project(2)
-    gram_copies = middle_gram(1, gram_copies)
-    laplacian(2, halo_copies)
-    rough_copies = start_gram(2, products(v_split[...], split3(lap_ref[...])))
-    copies = finish_scatter(2, copies)
-    gram_copies = spread_gram(1, gram_copies)
-    rough_copies = middle_gram(2, rough_copies)
+        expand_pair(2, i, parts)
+
+    start_gram(1, gram())
+    start_halo(2)
+    project(2)
+    middle_gram(1)
+    laplacian(2)
+    start_gram(2, products(v_split[...], split3(lap_ref[...])))
+    finish_scatter(2)
+    spread_gram(1)
+    middle_gram(2)
     rows = gram_piece(own_block)
     if per == 1:
         for h in range(halves):
-            finish_lon(2, h, copies)
-        coeffs = split3(fin[2, 0])
+            finish_lon(2, h)
+        coeffs = split3(load_block(2, 0))
         middle = products(coeffs, coeffs) * inverse_points
         g_out[2] = jnp.concatenate([middle, middle], axis=1)
     else:
         g_out[2] = jnp.zeros((k, b_count), F32)
-        copies = start_gather(2, copies)
-    rough = jnp.where(own_piece == 0, sum_gram(2, rough_copies), 0.0)
+        start_gather(2)
+    rough = jnp.where(own_piece == 0, sum_gram(2), 0.0)
     g_out[2, rows, :] = g_out[2, rows, :] + rough
-    plane_copies = start_plane(pack(g_out[2, :, :k]))
-    inverse = inverse_factor(finish_gram(1, gram_copies))
+    start_plane(pack(g_out[2, :, :k]))
+    inverse = inverse_factor(finish_gram(1))
     parts = factor_parts(inverse)
     for block in range(a_count // 2):
         at = slice(block * wide, (block + 1) * wide)
         out_ref[:, at] = times(parts, v_split[:, at])
-    middle = unpack(finish_plane(plane_copies))
+    middle = unpack(finish_plane())
     if per > 1:
-        for block in range(blocks):
-            wait_block(block, copies)
+        for i in range(pairs):
+            wait_pair(2, i)
         coeffs = split3(jnp.concatenate(
-            [fin[2, flip(own_block, block)] for block in range(blocks)], axis=1
+            [
+                fin[2, pl.ds(flip(own_block, block) * per, per)].reshape(k, b_count)
+                for block in range(blocks)
+            ], axis=1,
         ))
         middle = middle + products(coeffs, coeffs) * inverse_points
     half = times(parts, split3(middle))
     ray_ref[...] = products(split3(half), split3(inverse)) * inverse_points
-    for copy in pending:
-        copy.wait_send()
+    arrived(plane.at[pl.ds(1, n - 1)], c_sem.at[3])
+    for r in range(3):
+        arrived(rs.at[r, pl.ds(1, n - 1)], rs_s.at[r])
+        arrived(zr.at[r, pl.ds(1, m - 1)], z_s.at[r])
+        arrived(gr.at[r, pl.ds(1, n - 1)], gr_s.at[r])
+        arrived(gz.at[r, pl.ds(1, m - 1)], gz_s.at[r])
+        arrived(halo.at[r], h_s.at[r])
+        if r < 2 or per > 1:
+            arrived(fin.at[r, pl.ds(1, n - 1)], ag_s.at[r])
+        if r < 2:
+            arrived(other_pieces(r), ga_s.at[r])
 
 
 def write_out(x_ref, ray_ref, out_hbm, ray_hbm, sems):
     a_count, b_count = out_hbm.shape[1:]
-    copies = [pltpu.make_async_copy(ray_ref, ray_hbm, sems.at[a_count])]
+    ray_copy = pltpu.make_async_copy(ray_ref, ray_hbm, sems.at[0])
+    ray_copy.start()
     for a in range(a_count):
         at = pl.ds(a * b_count, b_count)
-        copies.append(pltpu.make_async_copy(x_ref.at[:, at], out_hbm.at[:, a, :], sems.at[a]))
-    for copy in copies:
-        copy.start()
-    for copy in copies:
-        copy.wait()
+        pltpu.make_async_copy(x_ref.at[:, at], out_hbm.at[:, a, :], sems.at[1]).start()
+    ray_copy.wait()
+    pltpu.make_async_copy(x_ref, x_ref, sems.at[1]).wait()
 
 
 def local(snapshots, land_sea, penalty, initial_basis):
@@ -583,14 +570,12 @@
             vmem((k, p), F32), vmem((k, p), F32), vmem((k, p), F32),
             vmem((k, p), F32), vmem((3 * k, p), BF16),
             vmem((3, blocks, k, b), F32), vmem((3, n, shard, b), F32), vmem((3, m, shard, b), F32),
-            vmem((3, blocks, k, b), F32), vmem((3, k, b), F32), vmem((3, n, k // blocks, b), F32),
+            vmem((3, n, shard, b), F32), vmem((3, k, b), F32), vmem((3, n, k // blocks, b), F32),
             vmem((3, m, k // blocks, b), F32), vmem((3, k, b), F32), vmem((n, k // 2, b), F32),
-            vmem((3, 2 * a * k // b, b), F32), vmem((3, 2, k, b), F32),
-            vmem((3, 2, 2 * a * k // b, b), F32),
-            sem((2,)), sem((blocks // 2, a)), sem((a,)),
-            sem((3, n)), sem((3, n)), sem((3, 2, m)), sem((3, 2, m)), sem((3, 2, n)), sem((3, 2, n)),
-            sem((3, n)), sem((3, n)), sem((3, m)), sem((3, m)), sem((3, blocks)), sem((3, blocks)),
-            sem((n,)), sem((n,)), sem((3, 4)), sem((3, 4)),
+            vmem((3, 2 * a * k // b, b), F32), vmem((3, 2 * k + 4 * a * k // b, b), F32),
+            sem((5,)), sem((blocks // 2, 2)),
+            sem((3,)), sem((3,)), sem((3,)), sem((3, 2)), sem((3,)), sem((3, blocks // 2)),
+            sem((3,)), sem((3,)), sem((3,)), sem((3,)), sem((2,)), sem((2,)), sem((3,)), sem((3,)),
         ],
         compiler_params=pltpu.CompilerParams(
             collective_id=0, has_side_effects=True, vmem_limit_bytes=60 * 1024 * 1024
@@ -602,7 +587,7 @@
         out_shape=(jax.ShapeDtypeStruct((k, a, b), F32), jax.ShapeDtypeStruct((k, k), F32)),
         in_specs=[vmem_spec, vmem_spec],
         out_specs=(any_spec, any_spec),
-        scratch_shapes=[sem((a + 1,))],
+        scratch_shapes=[sem((2,))],
         name="write_out",
     )(
         pltpu.with_memory_space_constraint(out, pltpu.VMEM),

time: 62.4 us -> 58.7 us (0.941)
  Pallas kernels: 61.5 us -> 57.7 us
    pallas_call x1, Pallas kernels: 60.5 us -> 56.9 us  [local(): pl.pallas_call(functools.partial(kernel, n, m, points), out_shape=(vmem((...]
where the time goes in v3:
time: 58.7 us; the launch traced here: 58.5 us
  Pallas kernels  57.7 us (98%)
  between operations  0.8 us (1%)
    pallas_call x1, Pallas kernels, local(): pl.pallas_call(functools.partial(kernel, n, m, points), out_shape=(vmem((...  56.9 us

profile of v3, /device:TPU:0, one launch (start us, length us, event | category | flops | bytes accessed | tf_op | source)
XLA Modules:
  0.0 58.5 jit_solution(10664557161134104127)
XLA Ops:
  0.6 56.9 %power_steps.1 = (f32[64,2048]{1,0:T(8,128)S(1)}, f32[64,64]{1,0:T(8,128)S(1)}) custom-call(f32[1024,16,128]{2,1,0:T(8,128)} %s_hbm.1, s32[16,128]{1,0:T(8,128)} %land_hbm.1, f32[16,128]{1,0:T(8,128)} %pen_hbm.1, f32[64,16,128]{2,1,0:T(8,128)} %v_hbm.1), custom_call_target="tpu_custom_call" | custom-call | tf_op jit(solution)/shard_map/power_steps/pallas_call | solution.py:561
  57.6 0.8 %write_out.1 = (f32[64,16,128]{2,1,0:T(8,128)}, f32[64,64]{1,0:T(8,128)}) custom-call(f32[64,2048]{1,0:T(8,128)S(1)} %get-tuple-element.4.x_ref, f32[64,64]{1,0:T(8,128)S(1)} %get-tuple-element.5.ray_ref), custom_call_target="tpu_custom_call" | custom-call | tf_op jit(solution)/shard_map/write_out/pallas_call | solution.py:585

commit v4 on v3

--- a/solution.py
+++ b/solution.py
@@ -124,7 +124,7 @@
     n, m, points, s_hbm, land_hbm, pen_hbm, v_hbm, out_ref, ray_ref,
     land_ref, pen_ref, s_full, s_high, s_mid, t_high, t_mid, field0, field1, field2, lap_ref, v_split,
     cbuf, rs, zr, fin, g_in, gr, gz, g_out, plane, edge, halo,
-    c_sem, s_sem, rs_s, rs_r, z_s, z_r, ag_s, ag_r, gr_s, gr_r, gz_s, gz_r, ga_s, ga_r, h_s, h_r,
+    c_sem, s_sem, out_sem, rs_r, z_r, ag_r, gr_r, gz_r, ga_r, h_r,
 ):
     lat = lax.axis_index("lat")
     lon = lax.axis_index("lon")
@@ -231,10 +231,10 @@
         right, left = (lat, lax.rem(lon + 1, m)), (lat, lax.rem(lon + m - 1, m))
         first, second = pl.ds(0, k), pl.ds(k, k)
         third, fourth = pl.ds(2 * k, edge_rows), pl.ds(2 * k + edge_rows, edge_rows)
-        send(x.at[:, part(a_count - 1)], halo.at[r, first], h_s.at[r], h_r.at[r], up)
-        send(x.at[:, part(0)], halo.at[r, second], h_s.at[r], h_r.at[r], down)
-        send(edge.at[r], halo.at[r, third], h_s.at[r], h_r.at[r], right)
-        send(edge.at[r], halo.at[r, fourth], h_s.at[r], h_r.at[r], left)
+        send(x.at[:, part(a_count - 1)], halo.at[r, first], out_sem.at[6], h_r.at[r], up)
+        send(x.at[:, part(0)], halo.at[r, second], out_sem.at[6], h_r.at[r], down)
+        send(edge.at[r], halo.at[r, third], out_sem.at[6], h_r.at[r], right)
+        send(edge.at[r], halo.at[r, fourth], out_sem.at[6], h_r.at[r], left)
 
     def widen(x):
         return jnp.concatenate(
@@ -317,7 +317,7 @@
                     rows = piece_rows(lax.rem(flip(lat, d), per))
                     send(
                         cbuf.at[r, 2 * i + e, rows], rs.at[r, d],
-                        rs_s.at[r], rs_r.at[r], to_lat(d),
+                        out_sem.at[0], rs_r.at[r], to_lat(d),
                     )
 
     def project(r):
@@ -337,7 +337,7 @@
             zr[r, lon, at, :] = total
             own = zr.at[r, lon, pl.ds(h * part_rows, part_rows)]
             for e in reversed(range(1, m)):
-                send(own, own, z_s.at[r], z_r.at[r, h], to_lon(e))
+                send(own, own, out_sem.at[1], z_r.at[r, h], to_lon(e))
 
     def finish_lon(r, h):
         arrived(zr.at[r, pl.ds(1, m - 1), pl.ds(h * part_rows, part_rows)], z_r.at[r, h])
@@ -355,7 +355,7 @@
                 block = d // per
                 send(
                     fin.at[r, own_piece, rows], fin.at[r, block * per + own_piece, rows],
-                    ag_s.at[r], ag_r.at[r, block // 2], to_lat(d),
+                    out_sem.at[2], ag_r.at[r, block // 2], to_lat(d),
                 )
 
     def wait_pair(r, i):
@@ -376,7 +376,7 @@
         for d in reversed(range(1, n)):
             send(
                 g_in.at[r, gram_piece(flip(own_block, d // per))], gr.at[r, lat],
-                gr_s.at[r], gr_r.at[r], to_lat(d),
+                out_sem.at[3], gr_r.at[r], to_lat(d),
             )
 
     def middle_gram(r):
@@ -386,7 +386,7 @@
             total = total + gr[r, d]
         gz[r, lon] = total
         for e in reversed(range(1, m)):
-            send(gz.at[r, lon], gz.at[r, lon], gz_s.at[r], gz_r.at[r], to_lon(e))
+            send(gz.at[r, lon], gz.at[r, lon], out_sem.at[4], gz_r.at[r], to_lon(e))
 
     def sum_gram(r):
         arrived(gz.at[r, pl.ds(1, m - 1)], gz_r.at[r])
@@ -400,7 +400,7 @@
         g_out[r, rows, :] = sum_gram(r)
         for block in reversed(range(1, blocks)):
             send(
-                g_out.at[r, rows], g_out.at[r, rows], ga_s.at[r], ga_r.at[r], to_lat(block * per)
+                g_out.at[r, rows], g_out.at[r, rows], out_sem.at[5], ga_r.at[r], to_lat(block * per)
             )
 
     def other_pieces(r):
@@ -413,10 +413,10 @@
     def start_plane(value):
         plane[lat] = value
         for d in reversed(range(1, n)):
-            send(plane.at[lat], plane.at[lat], c_sem.at[3], c_sem.at[4], to_lat(d))
+            send(plane.at[lat], plane.at[lat], out_sem.at[7], c_sem.at[3], to_lat(d))
 
     def finish_plane():
-        arrived(plane.at[pl.ds(1, n - 1)], c_sem.at[4])
+        arrived(plane.at[pl.ds(1, n - 1)], c_sem.at[3])
         total = plane[0]
         for d in range(1, n):
             total = total + plane[d]
@@ -491,26 +491,23 @@
     finish_scatter(2)
     spread_gram(1)
     middle_gram(2)
-    rows = gram_piece(own_block)
     if per == 1:
         for h in range(halves):
             finish_lon(2, h)
         coeffs = split3(load_block(2, 0))
-        middle = products(coeffs, coeffs) * inverse_points
-        g_out[2] = jnp.concatenate([middle, middle], axis=1)
+        start_plane(pack(products(coeffs, coeffs) * inverse_points))
     else:
-        g_out[2] = jnp.zeros((k, b_count), F32)
         start_gather(2)
-    rough = jnp.where(own_piece == 0, sum_gram(2), 0.0)
-    g_out[2, rows, :] = g_out[2, rows, :] + rough
-    start_plane(pack(g_out[2, :, :k]))
+    spread_gram(2)
     inverse = inverse_factor(finish_gram(1))
     parts = factor_parts(inverse)
+    turned = split3(inverse.T)
     for block in range(a_count // 2):
         at = slice(block * wide, (block + 1) * wide)
         out_ref[:, at] = times(parts, v_split[:, at])
-    middle = unpack(finish_plane())
-    if per > 1:
+    if per == 1:
+        middle = unpack(finish_plane())
+    else:
         for i in range(pairs):
             wait_pair(2, i)
         coeffs = split3(jnp.concatenate(
@@ -519,20 +516,22 @@
                 for block in range(blocks)
             ], axis=1,
         ))
-        middle = middle + products(coeffs, coeffs) * inverse_points
-    half = times(parts, split3(middle))
-    ray_ref[...] = products(split3(half), split3(inverse)) * inverse_points
-    arrived(plane.at[pl.ds(1, n - 1)], c_sem.at[3])
-    for r in range(3):
-        arrived(rs.at[r, pl.ds(1, n - 1)], rs_s.at[r])
-        arrived(zr.at[r, pl.ds(1, m - 1)], z_s.at[r])
-        arrived(gr.at[r, pl.ds(1, n - 1)], gr_s.at[r])
-        arrived(gz.at[r, pl.ds(1, m - 1)], gz_s.at[r])
-        arrived(halo.at[r], h_s.at[r])
-        if r < 2 or per > 1:
-            arrived(fin.at[r, pl.ds(1, n - 1)], ag_s.at[r])
-        if r < 2:
-            arrived(other_pieces(r), ga_s.at[r])
+        middle = products(coeffs, coeffs) * inverse_points
+    middle = middle + finish_gram(2)
+    half = factor_parts(times(parts, split3(middle)))
+    ray_ref[...] = times(half, turned) * inverse_points
+    gathers = 2
+    if per == 1:
+        arrived(plane.at[pl.ds(1, n - 1)], out_sem.at[7])
+    else:
+        gathers = 3
+    arrived(rs.at[:, pl.ds(1, n - 1)], out_sem.at[0])
+    arrived(zr.at[:, pl.ds(1, m - 1)], out_sem.at[1])
+    arrived(fin.at[pl.ds(0, gathers), pl.ds(1, n - 1)], out_sem.at[2])
+    arrived(gr.at[:, pl.ds(1, n - 1)], out_sem.at[3])
+    arrived(gz.at[:, pl.ds(1, m - 1)], out_sem.at[4])
+    arrived(g_out.at[:, pl.ds(gram_rows, k - gram_rows)], out_sem.at[5])
+    arrived(halo, out_sem.at[6])
 
 
 def write_out(x_ref, ray_ref, out_hbm, ray_hbm, sems):
@@ -573,9 +572,8 @@
             vmem((3, n, shard, b), F32), vmem((3, k, b), F32), vmem((3, n, k // blocks, b), F32),
             vmem((3, m, k // blocks, b), F32), vmem((3, k, b), F32), vmem((n, k // 2, b), F32),
             vmem((3, 2 * a * k // b, b), F32), vmem((3, 2 * k + 4 * a * k // b, b), F32),
-            sem((5,)), sem((blocks // 2, 2)),
-            sem((3,)), sem((3,)), sem((3,)), sem((3, 2)), sem((3,)), sem((3, blocks // 2)),
-            sem((3,)), sem((3,)), sem((3,)), sem((3,)), sem((2,)), sem((2,)), sem((3,)), sem((3,)),
+            sem((4,)), sem((blocks // 2, 2)), sem((8,)), sem((3,)), sem((3, 2)),
+            sem((3, blocks // 2)), sem((3,)), sem((3,)), sem((3,)), sem((3,)),
         ],
         compiler_params=pltpu.CompilerParams(
             collective_id=0, has_side_effects=True, vmem_limit_bytes=60 * 1024 * 1024

time: 58.7 us -> 58.5 us (level)
  no operation moved by 1% of the time
where the time goes in v4:
time: 58.5 us; the launch traced here: 58.3 us
  Pallas kernels  57.5 us (98%)
  between operations  0.8 us (1%)
    pallas_call x1, Pallas kernels, local(): pl.pallas_call(functools.partial(kernel, n, m, points), out_shape=(vmem((...  56.7 us

profile of v4, /device:TPU:0, one launch (start us, length us, event | category | flops | bytes accessed | tf_op | source)
XLA Modules:
  0.0 58.3 jit_solution(11970978987030322913)
XLA Ops:
  0.6 56.7 %power_steps.1 = (f32[64,2048]{1,0:T(8,128)S(1)}, f32[64,64]{1,0:T(8,128)S(1)}) custom-call(f32[1024,16,128]{2,1,0:T(8,128)} %s_hbm.1, s32[16,128]{1,0:T(8,128)} %land_hbm.1, f32[16,128]{1,0:T(8,128)} %pen_hbm.1, f32[64,16,128]{2,1,0:T(8,128)} %v_hbm.1), custom_call_target="tpu_custom_call" | custom-call | tf_op jit(solution)/shard_map/power_steps/pallas_call | solution.py:560
  57.4 0.8 %write_out.1 = (f32[64,16,128]{2,1,0:T(8,128)}, f32[64,64]{1,0:T(8,128)}) custom-call(f32[64,2048]{1,0:T(8,128)S(1)} %get-tuple-element.4.x_ref, f32[64,64]{1,0:T(8,128)S(1)} %get-tuple-element.5.ray_ref), custom_call_target="tpu_custom_call" | custom-call | tf_op jit(solution)/shard_map/write_out/pallas_call | solution.py:583
